TPU v7x, 512 devices: a whole 4x8x8 slice. The times are simulated.
512 devices in a mesh: src: 64 (over z_lo, y, core), sub: 8 (over x, z_hi).
Axes of the slice: x: 4, y: 8, z: 8 (z_hi: 2, z_lo: 4; z = z_hi * 4 + z_lo), core: 2. Of those that a mesh axis runs over, the one named last changes fastest.
Arguments:
- child_rhs: float32 [8, 1024, 16384], P('sub', None, 'src'), may hold values from -6 to 6
- root_rhs: float32 [2048, 16384], P('sub', 'src'), may hold values from -6 to 6
- child_inverse: bfloat16 [8, 1024, 1024], P('sub', 'src'), as said below
- coupling_block: bfloat16 [8, 1024, 1024], P('sub', 'src'), may hold values from -0.1875 to 0.1875
- root_inverse: bfloat16 [2048, 2048], P('sub', 'src'), as said below
- child_orders: int32 [8], P('sub'), may hold values from 716 to 1024, as said below
- coupling_rows: int32 [8, 1024], P('sub'), may hold values from 0 to 2047, as said below
Outputs:
- child_solution: float32 [8, 1024, 16384], P('sub', None, 'src')
- root_solution: float32 [2048, 16384], P('sub', 'src')
Inputs may be any that keep to these rules, and one draw needn't show every extreme that they name: Each child_inverse[j] is lower triangular: zero above the diagonal, diagonal entries between 0.8 and 1.25. `root_inverse`: lower triangular: zero above the diagonal, diagonal entries between 0.8 and 1.25. `coupling_rows`: each row holds 1024 distinct root rows in increasing order. `child_orders`: some child has order 1024.
All inputs are finite; a program needn't handle non-finite values.
Results may differ from a plain program's by a relative error of at most 0.0093.
Values may be sent and summed in bfloat16 or wider, within the bound.
No kernel may reach another device: no remote copies, remote signals or barrier semaphores. Data moves between devices by JAX's collectives and lax.ppermute only.
A program may use at most 64 MiB of HBM per device.

v0:
```python
import jax
import jax.numpy as jnp
from jax import lax
from jax.sharding import PartitionSpec as P


def sent_to_all(x, axis):
    length = lax.axis_size(axis)
    return lax.all_to_all(jnp.broadcast_to(x[None], (length, *x.shape)), axis, 0, 0, tiled=True)


def in_order(blocks, dim):
    lengths = list(blocks.shape[1:])
    lengths[dim] *= blocks.shape[0]
    return jnp.moveaxis(blocks, 0, dim).reshape(lengths)


def collect(x, axis, dim):
    blocks = sent_to_all(x, axis)
    return in_order(blocks, dim)


def in_blocks(x, dim, length):
    before, after = (x.shape[:dim], x.shape[dim + 1 :])
    return jnp.moveaxis(x.reshape(*before, length, -1, *after), dim, 0)


def sum_at_owner(x, axis, dim):
    length = lax.axis_size(axis)
    blocks = lax.all_to_all(in_blocks(x, dim, length), axis, 0, 0, tiled=True)
    return jnp.sum(blocks.astype(jnp.float32), axis=0)


def contract_rows(left, right):
    return lax.dot_general(
        left, right, (((0,), (0,)), ((), ())), preferred_element_type=jnp.float32
    )


def on_device(
    child_rhs, root_rhs, child_inverse, coupling_block, root_inverse, child_orders, coupling_rows
):
    inverse = child_inverse[0]
    coupling = coupling_block[0]
    coupling_index = coupling_rows[0]
    columns = child_rhs.shape[2]
    child_order = inverse.shape[1]
    root_order = root_inverse.shape[1] * lax.axis_size("src")
    alive = (lax.iota(jnp.int32, child_order) < child_orders[0])[:, None]
    child_source = jnp.where(alive, child_rhs[0], 0.0).astype(jnp.bfloat16)
    whole_inverse = lax.all_gather(inverse, "src", axis=0, tiled=True)
    whole_coupling = collect(coupling, "src", 0)
    forward = jnp.dot(whole_inverse, child_source, preferred_element_type=jnp.float32)
    child_solved = jnp.where(alive, forward, 0.0)
    solved_round = child_solved.astype(jnp.bfloat16)
    update = jnp.dot(whole_coupling, solved_round, preferred_element_type=jnp.float32)
    placed = jnp.zeros((root_order, columns), jnp.float32).at[coupling_index].add(update)
    share = sum_at_owner(placed.astype(jnp.bfloat16), "sub", 0)
    root_source = collect((root_rhs - share).astype(jnp.bfloat16), "sub", 0)
    root_rows = lax.all_gather(root_inverse, "src", axis=1, tiled=True)
    root_forward = jnp.dot(root_rows, root_source, preferred_element_type=jnp.float32)
    root_round = root_forward.astype(jnp.bfloat16)
    partial_root = contract_rows(root_rows, root_round)
    root_out = sum_at_owner(partial_root.astype(jnp.bfloat16), "sub", 0)
    rounded_all = collect(root_out.astype(jnp.bfloat16), "sub", 0)
    picked = rounded_all[coupling_index]
    pulled = contract_rows(whole_coupling, picked)
    residue = jnp.where(alive, child_solved - pulled, 0.0).astype(jnp.bfloat16)
    backward = contract_rows(whole_inverse, residue)
    child_out = jnp.where(alive, backward, 0.0)[None]
    return (child_out, root_out)


def solution(mesh):
    return jax.shard_map(
        on_device,
        mesh=mesh,
        in_specs=(
            P("sub", None, "src"),
            P("sub", "src"),
            P("sub", "src", None),
            P("sub", "src", None),
            P("sub", "src"),
            P("sub"),
            P("sub", None),
        ),
        out_specs=(P("sub", None, "src"), P("sub", "src")),
        check_vma=False,
    )
```

profile of v0, /device:TPU:73, one launch (start us, length us, event | category | flops | bytes accessed | tf_op | source)
XLA Modules:
  0.0 402.6 jit_solution(723256197187637208)
XLA Ops:
  7.2 0.7 all-gather.6.cloned.1.call-update
  7.9 2.3 broadcast_in_dim.62
  10.2 13.1 %all-to-all-start = ((bf16[64,16,1024]{2,1,0:T(8,128)(2,1)}), bf16[64,16,1024]{2,1,0:T(8,128)(2,1)S(1)}, u32[]{:S(2)}, u32[]{:S(2)}) async-start(bf16[64,16,1024]{2,1,0:T(8,128)(2,1)} %broadcast_in_dim.62), calls=%async_computation | async-start | bytes 4194304 | tf_op jit(solution)/shard_map/all_to_all | solution.py:9
  24.0 130.5 %all-gather.6.cloned.1.call-done = bf16[1,1024,1024]{2,1,0:T(8,128)(2,1)} async-done(((bf16[1,16,1024]{2,1,0:T(8,128)(2,1)}), bf16[1,1024,1024]{2,1,0:T(8,128)(2,1)}) %all-gather.6.cloned.1.call-update) | async-done | bytes 2097168 | tf_op jit(solution)/shard_map/all_gather | solution.py:51
  154.5 2.9 fusion.4
  157.4 2.0 convolution_bitcast_fusion
  159.4 2.6 copy.13
  162.0 7.0 %scatter_custom_fusion = f32[2048,256]{1,0:T(8,128)S(1)} fusion(s32[1024]{0:T(1024)S(1)} %bitcast.50, f32[1024,256]{1,0:T(8,128)} %copy.13, f32[]{:T(128)} %constant.3.clone.1), kind=kCustom, calls=%fused_computation.20 | custom fusion | flops 262144 | bytes 2097664 | tf_op jit(solution)/shard_map/scatter-add | solution.py:57
  169.0 1.1 convert_element_type.42
  170.1 9.9 %all-to-all-start.1 = ((bf16[8,256,256]{2,1,0:T(8,128)(2,1)}), bf16[8,256,256]{2,1,0:T(8,128)(2,1)S(1)}, u32[]{:S(2)}, u32[]{:S(2)}) async-start(bf16[8,256,256]{2,1,0:T(8,128)(2,1)} %bitcast.8), calls=%async_computation.1 | async-start | bytes 2097152 | tf_op jit(solution)/shard_map/all_to_all | solution.py:30
  180.1 0.7 all-gather.4.cloned.1.call-update
  180.8 30.2 %all-to-all-done.1 = bf16[8,256,256]{2,1,0:T(8,128)(2,1)S(1)} async-done(((bf16[8,256,256]{2,1,0:T(8,128)(2,1)}), bf16[8,256,256]{2,1,0:T(8,128)(2,1)S(1)}, u32[]{:S(2)}, u32[]{:S(2)}) %all-to-all-start.1) | async-done | bytes 1048608 | tf_op jit(solution)/shard_map/all_to_all | solution.py:30
  211.1 1.1 broadcast_in_dim.63
  212.2 3.6 all-to-all-start.2
  215.8 96.6 %all-gather.4.cloned.1.call-done = bf16[256,2048]{0,1:T(8,128)(2,1)} async-done(((bf16[256,32]{0,1:T(8,128)(2,1)}), bf16[256,2048]{0,1:T(8,128)(2,1)}) %all-gather.4.cloned.1.call-update) | async-done | bytes 1048592 | tf_op jit(solution)/shard_map/all_gather | solution.py:60
  312.4 2.8 convolution_convert_fusion
  315.3 42.1 %all_to_all.25 = bf16[8,256,256]{1,2,0:T(8,128)(2,1)S(1)} all-to-all(bf16[8,256,256]{1,2,0:T(8,128)(2,1)S(1)} %bitcast.46), channel_id=1, replica_groups=mesh['src'=64,'sub'=8] {'sub'}, dimensions={0} | all-to-all | bytes 2097152 | tf_op jit(solution)/shard_map/all_to_all | solution.py:30
  357.7 1.0 broadcast_in_dim.64
  358.7 3.6 all-to-all-start.4
  362.3 0.8 copy.18
  363.2 22.9 %all-to-all-done.4 = bf16[8,256,256]{2,1,0:T(8,128)(2,1)S(1)} async-done(((bf16[8,256,256]{2,1,0:T(8,128)(2,1)}), bf16[8,256,256]{2,1,0:T(8,128)(2,1)S(1)}, u32[]{:S(2)}, u32[]{:S(2)}) %all-to-all-start.4) | async-done | bytes 1048608 | tf_op jit(solution)/shard_map/all_to_all | solution.py:9
  386.1 5.0 %gather_fusion = bf16[1024,256]{1,0:T(8,128)(2,1)} fusion(bf16[2048,256]{1,0:T(8,128)(2,1)S(1)} %bitcast.43, s32[1024]{0:T(1024)S(1)} %broadcast_clamp_fusion), kind=kCustom, calls=%fused_computation | custom fusion | bytes 1052672 | tf_op jit(solution)/shard_map/gather | solution.py:66
  391.1 3.3 fusion.10
  394.4 1.3 copy.17
  (23 shorter events, 0.6 us)
Async XLA Ops:
  7.2 147.3 %all-gather.6.cloned.1.call-start = ((), (), s32[]{:S(2)}) async-start(), calls=%async_computation.6 | async-start | bytes 2129920 | tf_op jit(solution)/shard_map/all_gather | solution.py:51
  10.2 13.7 %copy-start.4 = (s32[1,1024]{1,0:T(1,128)S(1)}, s32[1,1024]{1,0:T(1,128)}, u32[]{:S(2)}) copy-start(s32[1,1024]{1,0:T(1,128)} %param.13) | copy-start | bytes 12292
  10.2 147.2 %all-to-all-start = ((bf16[64,16,1024]{2,1,0:T(8,128)(2,1)}), bf16[64,16,1024]{2,1,0:T(8,128)(2,1)S(1)}, u32[]{:S(2)}, u32[]{:S(2)}) async-start(bf16[64,16,1024]{2,1,0:T(8,128)(2,1)} %broadcast_in_dim.62), calls=%async_computation | async-start | bytes 4194304 | tf_op jit(solution)/shard_map/all_to_all | solution.py:9
  157.4 2.0 copy-start.2
  157.4 2.0 copy-start
  170.1 41.0 %copy-start.3 = (f32[256,256]{1,0:T(8,128)S(1)}, f32[256,256]{1,0:T(8,128)}, u32[]{:S(2)}) copy-start(f32[256,256]{1,0:T(8,128)} %param.8) | copy-start | bytes 786436
  170.1 40.8 %all-to-all-start.1 = ((bf16[8,256,256]{2,1,0:T(8,128)(2,1)}), bf16[8,256,256]{2,1,0:T(8,128)(2,1)S(1)}, u32[]{:S(2)}, u32[]{:S(2)}) async-start(bf16[8,256,256]{2,1,0:T(8,128)(2,1)} %bitcast.8), calls=%async_computation.1 | async-start | bytes 2097152 | tf_op jit(solution)/shard_map/all_to_all | solution.py:30
  180.0 132.4 %all-gather.4.cloned.1.call-start = ((), (), s32[]{:S(2)}) async-start(), calls=%async_computation.5 | async-start | bytes 1064960 | tf_op jit(solution)/shard_map/all_gather | solution.py:60
  212.2 100.2 %all-to-all-start.2 = ((bf16[8,256,256]{2,1,0:T(8,128)(2,1)}), bf16[8,256,256]{2,1,0:T(8,128)(2,1)S(1)}, u32[]{:S(2)}, u32[]{:S(2)}) async-start(bf16[8,256,256]{2,1,0:T(8,128)(2,1)} %broadcast_in_dim.63), calls=%async_computation.2 | async-start | bytes 2097152 | tf_op jit(solution)/shard_map/all_to_all | solution.py:9
  358.7 27.3 %all-to-all-start.4 = ((bf16[8,256,256]{2,1,0:T(8,128)(2,1)}), bf16[8,256,256]{2,1,0:T(8,128)(2,1)S(1)}, u32[]{:S(2)}, u32[]{:S(2)}) async-start(bf16[8,256,256]{2,1,0:T(8,128)(2,1)} %broadcast_in_dim.64), calls=%async_computation.4 | async-start | bytes 2097152 | tf_op jit(solution)/shard_map/all_to_all | solution.py:9
  386.1 5.0 %copy-start.1 = (bf16[64,16,1024]{2,1,0:T(8,128)(2,1)S(1)}, bf16[64,16,1024]{2,1,0:T(8,128)(2,1)}, u32[]{:S(2)}) copy-start(bf16[64,16,1024]{2,1,0:T(8,128)(2,1)} %copy-done) | copy-start | bytes 6291460
Sparse Core Ops, SparseCore 0:
  10.1 144.2 all-gather.5
  183.0 129.3 all-gather.3
where the time goes:
time: 403 us
  waiting for transfers between devices  282 us (70%)
  blocking collectives  42.1 us (10%)
  starting transfers between devices  30.2 us (7%)
  between operations  14.8 us (4%)
  local copies, waits for them, and re-layouts  14.3 us (4%)
  matrix products  11 us (3%)
  other arithmetic  8.5 us (2%)
    all_gather x1, waiting for transfers between devices, on_device(): whole_inverse = lax.all_gather(inverse, 'src', axis=0, tiled=True)  130 us
    all_gather x1, waiting for transfers between devices, on_device(): root_rows = lax.all_gather(root_inverse, 'src', axis=1, tiled=True)  96.6 us
    all_to_all x1, blocking collectives, sum_at_owner(): blocks = lax.all_to_all(in_blocks(x, dim, length), axis, 0, 0, tiled=True)  42.1 us
    all_to_all x1, waiting for transfers between devices, sum_at_owner(): blocks = lax.all_to_all(in_blocks(x, dim, length), axis, 0, 0, tiled=True)  30.2 us
    all_to_all x3, waiting for transfers between devices, sent_to_all(): lax.all_to_all(jnp.broadcast_to(x[None], (length, *x.shape)), axis, 0, 0,...  22.9 us
    all_to_all x3, starting transfers between devices, sent_to_all(): lax.all_to_all(jnp.broadcast_to(x[None], (length, *x.shape)), axis, 0, 0,...  20.2 us
    all_to_all x1, starting transfers between devices, sum_at_owner(): blocks = lax.all_to_all(in_blocks(x, dim, length), axis, 0, 0, tiled=True)  9.91 us
  transfers between devices with their start and end apart: 6, of which 4 were waited for; matrix products, arithmetic and copies ran while one was open for 2% of the time, Pallas kernels for 0%

commit v1 on v0

--- a/solution.py
+++ b/solution.py
@@ -57,7 +57,15 @@
     placed = jnp.zeros((root_order, columns), jnp.float32).at[coupling_index].add(update)
     share = sum_at_owner(placed.astype(jnp.bfloat16), "sub", 0)
     root_source = collect((root_rhs - share).astype(jnp.bfloat16), "sub", 0)
-    root_rows = lax.all_gather(root_inverse, "src", axis=1, tiled=True)
+    root_rows = jnp.concatenate(
+        jax.lax.all_to_all(
+            jnp.stack([root_inverse] * jax.lax.axis_size("src"), axis=0),
+            "src",
+            split_axis=0,
+            concat_axis=0,
+        ),
+        1,
+    )
     root_forward = jnp.dot(root_rows, root_source, preferred_element_type=jnp.float32)
     root_round = root_forward.astype(jnp.bfloat16)
     partial_root = contract_rows(root_rows, root_round)

time: 403 us -> 358 us (0.89)
  waiting for transfers between devices: 282 us -> 181 us
  blocking collectives: 42.1 us -> 105 us
  starting transfers between devices: 30.2 us -> 24.6 us
    all_gather x1 -> x0, waiting for transfers between devices: 96.6 us -> none  [on_device(): root_rows = lax.all_gather(root_inverse, 'src', axis=1, tiled=True)]
    all_to_all x0 -> x1, blocking collectives: none -> 33.5 us  [sent_to_all(): lax.all_to_all(jnp.broadcast_to(x[None], (length, *x.shape)), axis, 0, 0,...]
    all_to_all x1 -> x2, blocking collectives: 42.1 us -> 71.2 us  [sum_at_owner(): blocks = lax.all_to_all(in_blocks(x, dim, length), axis, 0, 0, tiled=True)]
    all_to_all x3 -> x2, starting transfers between devices: 20.2 us -> 16.6 us  [sent_to_all(): lax.all_to_all(jnp.broadcast_to(x[None], (length, *x.shape)), axis, 0, 0,...]
    all_to_all x3 -> x2, waiting for transfers between devices: 22.9 us -> 22.9 us  [sent_to_all(): lax.all_to_all(jnp.broadcast_to(x[None], (length, *x.shape)), axis, 0, 0,...]
  transfers between devices with their start and end apart: 6 -> 4, of which waited for: 4 -> 3; matrix products, arithmetic and copies ran while one was open for 2% -> 2% of each run, Pallas kernels for 0% -> 0%
where the time goes in v1:
time: 358 us; the launch traced here: 357 us
  waiting for transfers between devices  181 us (51%)
  blocking collectives  105 us (29%)
  starting transfers between devices  24.6 us (7%)
  between operations  14.9 us (4%)
  local copies, waits for them, and re-layouts  14.4 us (4%)
  matrix products  9.52 us (3%)
  other arithmetic  7.49 us (2%)
    all_gather x1, waiting for transfers between devices, on_device(): whole_inverse = lax.all_gather(inverse, 'src', axis=0, tiled=True)  131 us
    all_to_all x2, blocking collectives, sum_at_owner(): blocks = lax.all_to_all(in_blocks(x, dim, length), axis, 0, 0, tiled=True)  71.2 us
    all_to_all x1, blocking collectives, sent_to_all(): lax.all_to_all(jnp.broadcast_to(x[None], (length, *x.shape)), axis, 0, 0,...  33.5 us
    all_to_all x1, waiting for transfers between devices, on_device(): jax.lax.all_to_all(jnp.stack([root_inverse] * jax.lax.axis_size('src'), a...  27.3 us
    all_to_all x2, waiting for transfers between devices, sent_to_all(): lax.all_to_all(jnp.broadcast_to(x[None], (length, *x.shape)), axis, 0, 0,...  22.9 us
    all_to_all x2, starting transfers between devices, sent_to_all(): lax.all_to_all(jnp.broadcast_to(x[None], (length, *x.shape)), axis, 0, 0,...  16.6 us
    all_to_all x1, starting transfers between devices, on_device(): jax.lax.all_to_all(jnp.stack([root_inverse] * jax.lax.axis_size('src'), a...  7.9 us
  transfers between devices with their start and end apart: 4, of which 3 were waited for; matrix products, arithmetic and copies ran while one was open for 2% of the time, Pallas kernels for 0%

profile of v1, /device:TPU:73, one launch (start us, length us, event | category | flops | bytes accessed | tf_op | source)
XLA Modules:
  0.0 356.9 jit_solution(7640826835358834427)
XLA Ops:
  7.2 0.7 all-gather.3.cloned.1.call-update
  7.9 2.3 broadcast_in_dim.62
  10.2 13.1 %all-to-all-start = ((bf16[64,16,1024]{2,1,0:T(8,128)(2,1)}), bf16[64,16,1024]{2,1,0:T(8,128)(2,1)S(1)}, u32[]{:S(2)}, u32[]{:S(2)}) async-start(bf16[64,16,1024]{2,1,0:T(8,128)(2,1)} %broadcast_in_dim.62), calls=%async_computation | async-start | bytes 4194304 | tf_op jit(solution)/shard_map/all_to_all | solution.py:9
  24.0 130.6 %all-gather.3.cloned.1.call-done = bf16[1,1024,1024]{2,1,0:T(8,128)(2,1)} async-done(((bf16[1,16,1024]{2,1,0:T(8,128)(2,1)}), bf16[1,1024,1024]{2,1,0:T(8,128)(2,1)}) %all-gather.3.cloned.1.call-update) | async-done | bytes 2097168 | tf_op jit(solution)/shard_map/all_gather | solution.py:51
  154.6 2.9 fusion.4
  157.5 2.0 convolution_bitcast_fusion
  159.5 2.6 copy.14
  162.0 7.0 %scatter_custom_fusion = f32[2048,256]{1,0:T(8,128)S(1)} fusion(s32[1024]{0:T(1024)S(1)} %bitcast.55, f32[1024,256]{1,0:T(8,128)} %copy.14, f32[]{:T(128)} %constant.3.clone.1), kind=kCustom, calls=%fused_computation.20 | custom fusion | flops 262144 | bytes 2097664 | tf_op jit(solution)/shard_map/scatter-add | solution.py:57
  169.2 39.7 %all_to_all.30 = bf16[8,256,256]{2,1,0:T(8,128)(2,1)S(1)} all-to-all(bf16[8,256,256]{2,1,0:T(8,128)(2,1)S(1)} %bitcast.50), channel_id=1, replica_groups=mesh['src'=64,'sub'=8] {'sub'}, dimensions={0} | all-to-all | bytes 2097152 | tf_op jit(solution)/shard_map/all_to_all | solution.py:30
  208.9 1.1 stack.2
  210.0 7.9 %all-to-all-start.3 = ((bf16[64,256,32]{1,2,0:T(8,128)(2,1)}), bf16[64,256,32]{1,2,0:T(8,128)(2,1)S(1)}, u32[]{:S(2)}, u32[]{:S(2)}) async-start(bf16[64,256,32]{1,2,0:T(8,128)(2,1)} %stack.2), calls=%async_computation.3 | async-start | bytes 2097152 | tf_op jit(solution)/shard_map/all_to_all | solution.py:61
  217.9 0.1 convert_reduce_fusion.1
  218.1 27.3 %all-to-all-done.3 = bf16[64,256,32]{1,2,0:T(8,128)(2,1)S(1)} async-done(((bf16[64,256,32]{1,2,0:T(8,128)(2,1)}), bf16[64,256,32]{1,2,0:T(8,128)(2,1)S(1)}, u32[]{:S(2)}, u32[]{:S(2)}) %all-to-all-start.3) | async-done | bytes 1048608 | tf_op jit(solution)/shard_map/all_to_all | solution.py:61
  245.5 33.5 %all_to_all.31 = bf16[8,256,256]{2,1,0:T(8,128)(2,1)S(1)} all-to-all(bf16[8,256,256]{2,1,0:T(8,128)(2,1)S(1)} %broadcast_in_dim.63), channel_id=1, replica_groups=mesh['src'=64,'sub'=8] {'sub'}, dimensions={0} | all-to-all | bytes 2097152 | tf_op jit(solution)/shard_map/all_to_all | solution.py:9
  279.0 1.3 convolution_convert_fusion
  280.4 31.5 %all_to_all.32 = bf16[8,256,256]{1,2,0:T(8,128)(2,1)S(1)} all-to-all(bf16[8,256,256]{1,2,0:T(8,128)(2,1)S(1)} %bitcast.51), channel_id=1, replica_groups=mesh['src'=64,'sub'=8] {'sub'}, dimensions={0} | all-to-all | bytes 2097152 | tf_op jit(solution)/shard_map/all_to_all | solution.py:30
  311.8 0.1 convert_reduce_fusion
  312.1 1.0 broadcast_in_dim.64
  313.1 3.6 all-to-all-start.5
  316.7 0.8 copy.19
  317.5 22.9 %all-to-all-done.5 = bf16[8,256,256]{2,1,0:T(8,128)(2,1)S(1)} async-done(((bf16[8,256,256]{2,1,0:T(8,128)(2,1)}), bf16[8,256,256]{2,1,0:T(8,128)(2,1)S(1)}, u32[]{:S(2)}, u32[]{:S(2)}) %all-to-all-start.5) | async-done | bytes 1048608 | tf_op jit(solution)/shard_map/all_to_all | solution.py:9
  340.5 5.0 %gather_fusion = bf16[1024,256]{1,0:T(8,128)(2,1)} fusion(bf16[2048,256]{1,0:T(8,128)(2,1)S(1)} %bitcast.46, s32[1024]{0:T(1024)S(1)} %broadcast_clamp_fusion), kind=kCustom, calls=%fused_computation | custom fusion | bytes 1052672 | tf_op jit(solution)/shard_map/gather | solution.py:74
  345.4 3.3 fusion.10
  348.8 1.3 copy.18
  (23 shorter events, 0.5 us)
Async XLA Ops:
  7.2 147.4 %all-gather.3.cloned.1.call-start = ((), (), s32[]{:S(2)}) async-start(), calls=%async_computation.6 | async-start | bytes 2129920 | tf_op jit(solution)/shard_map/all_gather | solution.py:51
  10.2 13.7 %copy-start.5 = (s32[1,1024]{1,0:T(1,128)S(1)}, s32[1,1024]{1,0:T(1,128)}, u32[]{:S(2)}) copy-start(s32[1,1024]{1,0:T(1,128)} %param.13) | copy-start | bytes 12292
  10.2 147.3 %all-to-all-start = ((bf16[64,16,1024]{2,1,0:T(8,128)(2,1)}), bf16[64,16,1024]{2,1,0:T(8,128)(2,1)S(1)}, u32[]{:S(2)}, u32[]{:S(2)}) async-start(bf16[64,16,1024]{2,1,0:T(8,128)(2,1)} %broadcast_in_dim.62), calls=%async_computation | async-start | bytes 4194304 | tf_op jit(solution)/shard_map/all_to_all | solution.py:9
  157.5 2.0 copy-start.2
  157.5 2.0 copy-start
  169.1 39.8 %copy-start.4 = (bf16[256,32]{0,1:T(8,128)(2,1)S(1)}, bf16[256,32]{0,1:T(8,128)(2,1)}, u32[]{:S(2)}) copy-start(bf16[256,32]{0,1:T(8,128)(2,1)} %param.11) | copy-start | bytes 49156
  208.9 9.2 %copy-start.3 = (f32[256,256]{1,0:T(8,128)S(1)}, f32[256,256]{1,0:T(8,128)}, u32[]{:S(2)}) copy-start(f32[256,256]{1,0:T(8,128)} %param.8) | copy-start | bytes 786436
  210.0 35.4 %all-to-all-start.3 = ((bf16[64,256,32]{1,2,0:T(8,128)(2,1)}), bf16[64,256,32]{1,2,0:T(8,128)(2,1)S(1)}, u32[]{:S(2)}, u32[]{:S(2)}) async-start(bf16[64,256,32]{1,2,0:T(8,128)(2,1)} %stack.2), calls=%async_computation.3 | async-start | bytes 2097152 | tf_op jit(solution)/shard_map/all_to_all | solution.py:61
  313.1 27.3 %all-to-all-start.5 = ((bf16[8,256,256]{2,1,0:T(8,128)(2,1)}), bf16[8,256,256]{2,1,0:T(8,128)(2,1)S(1)}, u32[]{:S(2)}, u32[]{:S(2)}) async-start(bf16[8,256,256]{2,1,0:T(8,128)(2,1)} %broadcast_in_dim.64), calls=%async_computation.5 | async-start | bytes 2097152 | tf_op jit(solution)/shard_map/all_to_all | solution.py:9
  340.4 5.0 %copy-start.1 = (bf16[64,16,1024]{2,1,0:T(8,128)(2,1)S(1)}, bf16[64,16,1024]{2,1,0:T(8,128)(2,1)}, u32[]{:S(2)}) copy-start(bf16[64,16,1024]{2,1,0:T(8,128)(2,1)} %copy-done) | copy-start | bytes 6291460
Sparse Core Ops, SparseCore 0:
  10.1 144.3 all-gather.2
